TPU v7x, 512 devices: a whole 4x4x16 slice. The times are simulated.
512 devices in a mesh: chan: 32 (over y, z_lo), ctx: 16 (over z_hi, x, core).
Axes of the slice: x: 4, y: 4, z: 16 (z_hi: 2, z_lo: 8; z = z_hi * 8 + z_lo), core: 2. Of those that a mesh axis runs over, the one named last changes fastest.
Arguments:
- inputs: bfloat16 [2048, 8192], P('ctx', 'chan'), may hold values from -6 to 6
- gate: bfloat16 [2048, 8192], P('ctx', 'chan'), may hold values from -200 to 200
- filter_taps: bfloat16 [2048, 8192], P('ctx', 'chan'), may hold values from -4 to 4, as said below
- cotangent: bfloat16 [2048, 8192], P('ctx', 'chan'), may hold values from -6 to 6
Outputs:
- output: bfloat16 [2048, 8192], P('ctx', 'chan')
- gate_grad: bfloat16 [2048, 8192], P('ctx', 'chan')
- input_grad: bfloat16 [2048, 8192], P('ctx', 'chan')
- filter_grad: float32 [2048, 8192], P('ctx', 'chan')
Inputs may be any that keep to these rules, and one draw needn't show every extreme that they name: `filter_taps`: each channel's filter taps shrink with the lag at a rate of their own.
All inputs are finite; a program needn't handle non-finite values.
Results may differ from a plain program's by a relative error of at most 0.005.
Values may be sent and summed in bfloat16 or wider, within the bound.
A program may use at most 64 MiB of HBM per device.

v0:
```python
import math

import jax
import jax.numpy as jnp
from jax import lax
from jax.sharding import PartitionSpec as P

HIGHEST = lax.Precision.HIGHEST
EPSILON = 1e-06


def tables(block_len):
    period = 2 * block_len
    offsets = jnp.arange(block_len, dtype=jnp.int32)
    harmonics = jnp.arange(block_len + 1, dtype=jnp.int32)
    samples = jnp.arange(period, dtype=jnp.int32)
    radians = math.pi / block_len
    angles = jnp.mod(harmonics[:, None] * offsets[None, :], period).astype(jnp.float32) * radians
    back_angles = (
        jnp.mod(samples[:, None] * harmonics[None, :], period).astype(jnp.float32) * radians
    )
    weights = (
        jnp.where((harmonics == 0) | (harmonics == block_len), 1.0, 2.0).astype(jnp.float32)
        / period
    )
    return (
        jnp.cos(angles),
        jnp.sin(angles),
        jnp.cos(back_angles) * weights[None, :],
        jnp.sin(back_angles) * weights[None, :],
    )


def spectrum(series, block_len, fwd_cos, fwd_sin):
    number = series.shape[0] // block_len
    blocks = series.astype(jnp.float32).reshape(number, block_len, series.shape[1])
    real_part = jnp.einsum("kn,bnc->bkc", fwd_cos, blocks, precision=HIGHEST)
    imag_part = -jnp.einsum("kn,bnc->bkc", fwd_sin, blocks, precision=HIGHEST)
    return (real_part, imag_part)


def inverse_many(real_part, imag_part, inv_cos, inv_sin):
    return jnp.einsum("mk,skc->smc", inv_cos, real_part, precision=HIGHEST) - jnp.einsum(
        "mk,skc->smc", inv_sin, imag_part, precision=HIGHEST
    )


def select(spectra, position):
    number = spectra[0].shape[0]
    inside = jnp.logical_and(position >= 0, position < number)
    clipped = jnp.clip(position, 0, number - 1)
    real_part = lax.dynamic_index_in_dim(spectra[0], clipped, 0, keepdims=False)
    imag_part = lax.dynamic_index_in_dim(spectra[1], clipped, 0, keepdims=False)
    return (jnp.where(inside, real_part, 0.0), jnp.where(inside, imag_part, 0.0))


def product(left, right, conjugate):
    if conjugate:
        return (left[0] * right[0] + left[1] * right[1], left[0] * right[1] - left[1] * right[0])
    return (left[0] * right[0] - left[1] * right[1], left[0] * right[1] + left[1] * right[0])


def forward_terms(taps_spec, input_spec, first_block, targets):
    empty = jnp.zeros((targets,) + taps_spec[0].shape[1:], jnp.float32)

    def forward_advance(offset, totals):
        reals, imags = totals
        kernel = select(taps_spec, offset)
        for target in range(targets):
            addend = product(kernel, select(input_spec, first_block - 1 + target - offset), False)
            reals = reals.at[target].add(addend[0])
            imags = imags.at[target].add(addend[1])
        return (reals, imags)

    return lax.fori_loop(0, taps_spec[0].shape[0], forward_advance, (empty, empty))


def backward_terms(taps_spec, inner_spec, first_block, targets):
    empty = jnp.zeros((targets,) + taps_spec[0].shape[1:], jnp.float32)

    def backward_advance(offset, totals):
        reals, imags = totals
        kernel = select(taps_spec, offset)
        for target in range(targets):
            addend = product(kernel, select(inner_spec, first_block + target + offset), True)
            reals = reals.at[target].add(addend[0])
            imags = imags.at[target].add(addend[1])
        return (reals, imags)

    return lax.fori_loop(0, taps_spec[0].shape[0], backward_advance, (empty, empty))


def owner_terms(input_spec, inner_spec, first_block, targets):
    empty = jnp.zeros((targets,) + input_spec[0].shape[1:], jnp.float32)

    def owner_advance(later, totals):
        reals, imags = totals
        grads = select(inner_spec, later)
        for target in range(targets):
            addend = product(select(input_spec, later - first_block - target), grads, True)
            reals = reals.at[target].add(addend[0])
            imags = imags.at[target].add(addend[1])
        return (reals, imags)

    return lax.fori_loop(0, input_spec[0].shape[0], owner_advance, (empty, empty))


def local(inputs, gate, filter_taps, cotangent):
    row_count, local_chan = inputs.shape
    block_len = min(128, row_count)
    slot_count = row_count // block_len
    first_block = lax.axis_index("ctx") * slot_count
    seq_total = row_count * lax.axis_size("ctx")
    fwd_cos, fwd_sin, inv_cos, inv_sin = tables(block_len)
    all_taps = lax.all_gather(filter_taps, "ctx", axis=0, tiled=True)
    taps_spec = spectrum(all_taps, block_len, fwd_cos, fwd_sin)
    all_inputs = lax.all_gather(inputs, "ctx", axis=0, tiled=True)
    input_spec = spectrum(all_inputs, block_len, fwd_cos, fwd_sin)
    conv_real, conv_imag = forward_terms(taps_spec, input_spec, first_block, slot_count + 1)
    waves = inverse_many(conv_real, conv_imag, inv_cos, inv_sin)
    convolved = (waves[1:, :block_len] + waves[:-1, block_len:]).reshape(row_count, local_chan)
    gate_wide = gate.astype(jnp.float32)
    upstream = cotangent.astype(jnp.float32)
    mixed = gate_wide * convolved
    squares, projection = lax.psum(
        (jnp.sum(mixed * mixed, axis=1), jnp.sum(upstream * mixed, axis=1)), "chan"
    )
    channels = local_chan * lax.axis_size("chan")
    inv_rms = lax.rsqrt(squares / channels + EPSILON)[:, None]
    output = (mixed * inv_rms).astype(jnp.bfloat16)
    d_mixed = inv_rms * upstream - mixed * inv_rms**3 * projection[:, None] / channels
    gate_grad = (d_mixed * convolved).astype(jnp.bfloat16)
    d_inner = (d_mixed * gate_wide).astype(jnp.bfloat16)
    all_inner = lax.all_gather(d_inner, "ctx", axis=0, tiled=True)
    inner_spec = spectrum(all_inner, block_len, fwd_cos, fwd_sin)
    back_real, back_imag = backward_terms(taps_spec, inner_spec, first_block, slot_count + 1)
    waves = inverse_many(back_real, back_imag, inv_cos, inv_sin)
    input_grad = (
        (waves[:-1, :block_len] + waves[1:, block_len:])
        .reshape(row_count, local_chan)
        .astype(jnp.bfloat16)
    )
    lag_real, lag_imag = owner_terms(input_spec, inner_spec, first_block, slot_count + 1)
    waves = inverse_many(lag_real, lag_imag, inv_cos, inv_sin)
    filter_sum = (waves[:-1, :block_len] + waves[1:, block_len:]).reshape(row_count, local_chan)
    filter_grad = filter_sum / math.sqrt(seq_total)
    return (output, gate_grad, input_grad, filter_grad)


def solution(mesh):
    in_specs = (P("ctx", "chan"), P("ctx", "chan"), P("ctx", "chan"), P("ctx", "chan"))
    out_specs = (P("ctx", "chan"), P("ctx", "chan"), P("ctx", "chan"), P("ctx", "chan"))
    return jax.shard_map(local, mesh=mesh, in_specs=in_specs, out_specs=out_specs, check_vma=False)
```

profile of v0, /device:TPU:1, one launch (start us, length us, event | category | flops | bytes accessed | tf_op | source)
XLA Modules:
  0.0 500.6 jit_solution(9985710225990442809)
XLA Ops:
  10.6 84.2 %all-gather.6.cloned.1.call-done = bf16[2048,256]{1,0:T(8,128)(2,1)} async-done(((bf16[128,256]{1,0:T(8,128)(2,1)}), bf16[2048,256]{1,0:T(8,128)(2,1)}) %all-gather.6.cloned.1.call-update) | async-done | bytes 1048592 | tf_op jit(solution)/shard_map/all_gather | solution.py:117
  94.8 4.0 convolution_bitcast_fusion.1
  98.8 2.6 negate_bitcast_fusion.1
  101.5 65.2 %all-gather.4.cloned.1.call-done = bf16[2048,256]{1,0:T(8,128)(2,1)} async-done(((bf16[128,256]{1,0:T(8,128)(2,1)}), bf16[2048,256]{1,0:T(8,128)(2,1)}) %all-gather.4.cloned.1.call-update) | async-done | bytes 1048592 | tf_op jit(solution)/shard_map/all_gather | solution.py:115
  166.7 2.6 convolution_bitcast_fusion.2
  169.3 2.6 negate_bitcast_fusion.2
  172.0 38.1 %while.63 = (s32[]{:T(128)}, f32[2,129,256]{2,1,0:T(8,128)S(1)}, f32[2,129,256]{2,1,0:T(8,128)S(1)}, f32[16,129,256]{2,1,0:T(8,128)S(1)}, s32[]{:T(128)}, /*inde...) while((s32[]{:T(128)}, f32[2,129,256]{2,1,0:T(8,128)S(1)}, ...), condition=%wide.region_1.2_spmd, body=%wide.region_0.1_spmd.sunk | while | flops 792593 | bytes 2185508 | solution.py:75
  210.1 1.4 fusion.19
  211.5 1.5 fusion.8
  213.0 102.0 %all-reduce = (f32[128]{0:T(128)S(1)}, f32[128]{0:T(128)S(1)}) all-reduce(f32[128]{0:T(128)S(1)} %get-tuple-element.897, f32[128]{0:T(128)S(1)} %get-tuple-element.896), channel_id=1, replica_groups=mesh['chan'=32,'ctx'=16] {'chan'}, use_global_device_ids=true, to_apply=%region_3.4 | all-reduce | flops 256 | bytes 2048 | tf_op jit(solution)/shard_map/psum | solution.py:125
  317.3 84.4 %all-gather.8.cloned.1.call-done = bf16[2048,256]{0,1:T(8,128)(2,1)} async-done(((bf16[128,256]{0,1:T(8,128)(2,1)}), bf16[2048,256]{0,1:T(8,128)(2,1)}) %all-gather.8.cloned.1.call-update) | async-done | bytes 1048592 | tf_op jit(solution)/shard_map/all_gather | solution.py:134
  401.7 1.5 copy.16
  403.2 2.6 convolution_bitcast_fusion
  405.8 2.7 negate_bitcast_fusion
  408.6 40.0 %while.65 = (s32[]{:T(128)}, f32[2,129,256]{2,1,0:T(8,128)S(1)}, f32[2,129,256]{2,1,0:T(8,128)S(1)}, s32[]{:T(128)}, f32[16,129,256]{2,1,0:T(8,128)}, /*index=5*...) while((s32[]{:T(128)}, f32[2,129,256]{2,1,0:T(8,128)S(1)}, ...), condition=%wide.region_9.10_spmd, body=%wide.region_8.9_spmd.sunk | while | flops 792593 | bytes 2171172 | solution.py:105
  409.8 1.2 fusion.131
  414.8 1.2 fusion.131
  417.3 1.2 fusion.131
  419.8 1.2 fusion.131
  448.6 1.4 fusion.15
  450.0 1.5 fusion.6
  452.3 38.1 %while.64 = (s32[]{:T(128)}, f32[2,129,256]{2,1,0:T(8,128)S(1)}, f32[2,129,256]{2,1,0:T(8,128)S(1)}, f32[16,129,256]{2,1,0:T(8,128)S(1)}, s32[]{:T(128)}, /*inde...) while((s32[]{:T(128)}, f32[2,129,256]{2,1,0:T(8,128)S(1)}, ...), condition=%wide.region_7.8_spmd, body=%wide.region_6.7_spmd.sunk | while | flops 792593 | bytes 2185508 | solution.py:90
  490.4 1.4 fusion.17
  491.8 1.5 fusion.7
  (120 shorter events, 116.1 us)
Async XLA Ops:
  7.2 87.7 %all-gather.6.cloned.1.call-start = ((), (), s32[]{:S(2)}) async-start(), calls=%async_computation.1 | async-start | bytes 1114112 | tf_op jit(solution)/shard_map/all_gather | solution.py:117
  7.9 158.8 %all-gather.4.cloned.1.call-start = ((), (), s32[]{:S(2)}) async-start(), calls=%async_computation | async-start | bytes 1114112 | tf_op jit(solution)/shard_map/all_gather | solution.py:115
  8.6 393.1 %all-gather.8.cloned.1.call-start = ((), (), s32[]{:S(2)}) async-start(), calls=%async_computation.2 | async-start | bytes 1114112 | tf_op jit(solution)/shard_map/all_gather | solution.py:134
  94.8 4.0 copy-start
  166.7 2.6 copy-start.1
Sparse Core Ops, SparseCore 0:
  11.3 83.4 all-gather.5
  98.1 68.5 all-gather.3
  315.9 85.7 all-gather.7
where the time goes:
time: 503 us; the launch traced here: 501 us
  waiting for transfers between devices  235 us (47%)
  other arithmetic  114 us (23%)
  blocking collectives  102 us (20%)
  matrix products  25.9 us (5%)
  between operations  13.9 us (3%)
  local copies, waits for them, and re-layouts  6.49 us (1%)
    psum x1, blocking collectives, local(): lax.psum((jnp.sum(mixed * mixed, axis=1), jnp.sum(upstream * mixed, axis=...  102 us
    all_gather x1, waiting for transfers between devices, local(): all_inner = lax.all_gather(d_inner, 'ctx', axis=0, tiled=True)  84.4 us
    all_gather x1, waiting for transfers between devices, local(): all_inputs = lax.all_gather(inputs, 'ctx', axis=0, tiled=True)  84.2 us
    all_gather x1, waiting for transfers between devices, local(): all_taps = lax.all_gather(filter_taps, 'ctx', axis=0, tiled=True)  65.2 us
    scatter-add x32, other arithmetic, owner_advance(): imags = imags.at[target].add(addend[1])  39.1 us
    scatter-add x32, other arithmetic, backward_advance(): imags = imags.at[target].add(addend[1])  37.3 us
    scatter-add x32, other arithmetic, forward_advance(): imags = imags.at[target].add(addend[1])  37.3 us
  transfers between devices with their start and end apart: 3, of which 3 were waited for; matrix products, arithmetic and copies ran while one was open for 2% of the time, Pallas kernels for 0%

commit v1 on v0

v1 whole, which is shorter than its diff:
```python
import functools
import math

import jax
import jax.numpy as jnp
import ml_dtypes
import numpy as np
from jax import lax
from jax.experimental import pallas as pl
from jax.experimental.pallas import tpu as pltpu
from jax.sharding import PartitionSpec as P

EPSILON = 1e-06
MESH = pl.DeviceIdType.MESH
BF16 = jnp.bfloat16
F32 = jnp.float32


def split_table(table):
    head = table.astype(ml_dtypes.bfloat16)
    rest = (table - head.astype(np.float64)).astype(ml_dtypes.bfloat16)
    return head, rest


def dft_tables(n):
    k = np.arange(n)
    t = np.arange(n)
    angles = np.mod(np.outer(t, k), 2 * n) * (math.pi / n)
    alternate = np.where(t % 2 == 0, 1.0, -1.0)
    sines = -np.sin(angles)
    sines[:, 0] = alternate
    fwd = np.concatenate([np.cos(angles), sines], axis=1)
    weights = np.where(k == 0, 1.0, 2.0) / (2 * n)
    inv = np.concatenate(
        [np.cos(angles) * weights[None, :], sines * weights[None, :]], axis=1
    ).T
    return split_table(fwd) + split_table(inv)


def kernel(
    nb, nchan,
    x_ref, g_ref, h_ref, c_ref, fhi_ref, flo_ref, ihi_ref, ilo_ref,
    out_ref, gg_ref, ig_ref, fg_ref,
    s1, r1, s2, r2, s3, r3, s4, r4, stats,
    xre, xim, kre, kre2, kim, vre, vim, qre, qim,
    send_sems, recv_sems, stat_send, stat_recv,
):
    me = lax.axis_index("ctx")
    mc = lax.axis_index("chan")
    n, local_chan = x_ref.shape
    cb = local_chan // nb
    rows = nb * cb
    channels = local_chan * nchan

    barrier = pltpu.get_barrier_semaphore()

    def greet_ctx(k, _):
        pl.semaphore_signal(
            barrier, inc=1, device_id={"ctx": lax.rem(me + k, nb)}, device_id_type=MESH
        )
        return 0

    def greet_chan(k, _):
        pl.semaphore_signal(
            barrier, inc=1, device_id={"chan": lax.rem(mc + k, nchan)}, device_id_type=MESH
        )
        return 0

    lax.fori_loop(1, nb, greet_ctx, 0)
    lax.fori_loop(1, nchan, greet_chan, 0)

    def turned(ref):
        return ref[...].astype(F32).T

    s1[:, 0] = turned(x_ref).astype(BF16).reshape(nb, cb, n)
    s1[:, 1] = turned(h_ref).astype(BF16).reshape(nb, cb, n)
    pl.semaphore_wait(barrier, nb + nchan - 2)

    def exchange(phase, src, dst, k):
        return pltpu.make_async_remote_copy(
            src_ref=src.at[lax.rem(me + k, nb)],
            dst_ref=dst.at[me],
            send_sem=send_sems.at[phase, k],
            recv_sem=recv_sems.at[phase, k],
            device_id={"ctx": lax.rem(me + k, nb)},
            device_id_type=MESH,
        )

    def start_exchange(phase, src, dst):
        def step(k, _):
            exchange(phase, src, dst, k).start()
            return 0

        lax.fori_loop(1, nb, step, 0)
        dst[me] = src[me]

    def arrived(phase, src, dst, k):
        return pltpu.make_async_remote_copy(
            src_ref=src.at[lax.rem(me + nb - k, nb)],
            dst_ref=dst.at[lax.rem(me + nb - k, nb)],
            send_sem=send_sems.at[phase, k],
            recv_sem=recv_sems.at[phase, k],
            device_id={"ctx": lax.rem(me + nb - k, nb)},
            device_id_type=MESH,
        )

    def finish_exchange(phase, src, dst):
        def step(k, _):
            arrived(phase, src, dst, k).wait_recv()
            return 0

        lax.fori_loop(1, nb, step, 0)

    def sent(phase, src, dst):
        def step(k, _):
            exchange(phase, src, dst, k).wait_send()
            return 0

        lax.fori_loop(1, nb, step, 0)

    lane = lax.broadcasted_iota(jnp.int32, (1, 1, n), 2)
    alternate = jnp.where(lax.rem(lane, 2) == 0, 1.0, -1.0).astype(F32)
    first = lane == 0

    def spectrum(block):
        wide = jnp.dot(block, fhi_ref[...], preferred_element_type=F32) + jnp.dot(
            block, flo_ref[...], preferred_element_type=F32
        )
        return wide[:, :n].reshape(nb, cb, n), wide[:, n:].reshape(nb, cb, n)

    def inverse():
        def half(part, lo, hi):
            head = part.astype(BF16)
            rest = (part - head.astype(F32)).astype(BF16)
            return (
                jnp.dot(head, ihi_ref[lo:hi, :], preferred_element_type=F32)
                + jnp.dot(head, ilo_ref[lo:hi, :], preferred_element_type=F32)
                + jnp.dot(rest, ihi_ref[lo:hi, :], preferred_element_type=F32)
            )

        return half(qre[...].reshape(rows, n), 0, n) + half(qim[...].reshape(rows, n), n, 2 * n)

    def set_kernel(re, im):
        kre[...] = re
        kre2[...] = jnp.where(first, im, re)
        kim[...] = jnp.where(first, 0.0, im)

    def correlate():
        for d in range(nb):
            re, im = vre[d:], vim[d:]
            a, a2, b = kre[d : d + 1], kre2[d : d + 1], kim[d : d + 1]
            new_re = a * re + b * im
            new_im = a2 * im - b * re
            if d == 0:
                qre[...] = new_re
                qim[...] = new_im
            else:
                qre[: nb - d] += new_re
                qim[: nb - d] += new_im

    start_exchange(0, s1, r1)
    gate = turned(g_ref)
    upstream = turned(c_ref)
    finish_exchange(0, s1, r1)

    x_re, x_im = spectrum(r1[:, 0].reshape(rows, n))
    xre[...] = x_re
    xim[...] = x_im
    h_re, h_im = spectrum(r1[:, 1].reshape(rows, n))
    zero = jnp.zeros((1, cb, n), F32)
    set_kernel(
        h_re + alternate * jnp.concatenate([zero, h_re[:-1]], axis=0),
        h_im + alternate * jnp.concatenate([zero, h_im[:-1]], axis=0),
    )
    for d in range(nb):
        re, im = xre[: nb - d], xim[: nb - d]
        a, a2, b = kre[d : d + 1], kre2[d : d + 1], kim[d : d + 1]
        new_re = a * re - b * im
        new_im = b * re + a2 * im
        if d == 0:
            qre[...] = new_re
            qim[...] = new_im
        else:
            qre[d:] += new_re
            qim[d:] += new_im
    s2[...] = inverse().astype(BF16).reshape(nb, cb, n)
    start_exchange(1, s2, r2)
    finish_exchange(1, s2, r2)

    convolved = r2[...].reshape(rows, n).astype(F32)
    mixed = gate * convolved
    stats[mc, 0:1, :] = jnp.sum(mixed * mixed, axis=0, keepdims=True)
    stats[mc, 1:2, :] = jnp.sum(upstream * mixed, axis=0, keepdims=True)

    def stat_copy(k):
        return pltpu.make_async_remote_copy(
            src_ref=stats.at[mc],
            dst_ref=stats.at[mc],
            send_sem=stat_send.at[k],
            recv_sem=stat_recv.at[k],
            device_id={"chan": lax.rem(mc + k, nchan)},
            device_id_type=MESH,
        )

    def stat_start(k, _):
        stat_copy(k).start()
        return 0

    def stat_wait(k, _):
        source = lax.rem(mc + nchan - k, nchan)
        pltpu.make_async_remote_copy(
            src_ref=stats.at[source],
            dst_ref=stats.at[source],
            send_sem=stat_send.at[k],
            recv_sem=stat_recv.at[k],
            device_id={"chan": source},
            device_id_type=MESH,
        ).wait_recv()
        return 0

    def stat_sent(k, _):
        stat_copy(k).wait_send()
        return 0

    lax.fori_loop(1, nchan, stat_start, 0)
    lax.fori_loop(1, nchan, stat_wait, 0)
    totals = jnp.sum(stats[...], axis=0)
    inv_rms = lax.rsqrt(totals[0:1] / channels + EPSILON)
    d_mixed = inv_rms * upstream - mixed * (inv_rms**3 * totals[1:2] / channels)
    s3[...] = (d_mixed * gate).astype(BF16).reshape(nb, cb, n)
    start_exchange(2, s3, r3)
    out_ref[...] = (mixed * inv_rms).T.astype(BF16)
    gg_ref[...] = (d_mixed * convolved).T.astype(BF16)
    finish_exchange(2, s3, r3)

    d_re, d_im = spectrum(r3[...].reshape(rows, n))
    vre[...] = d_re
    vim[...] = d_im
    correlate()
    s4[:, 0] = inverse().astype(BF16).reshape(nb, cb, n)
    set_kernel(xre[...], xim[...])
    vre[: nb - 1] += alternate * vre[1:]
    vim[: nb - 1] += alternate * vim[1:]
    correlate()
    s4[:, 1] = (inverse() * (1.0 / math.sqrt(nb * n))).astype(BF16).reshape(nb, cb, n)
    start_exchange(3, s4, r4)
    sent(0, s1, r1)
    sent(1, s2, r2)
    lax.fori_loop(1, nchan, stat_sent, 0)
    sent(2, s3, r3)
    finish_exchange(3, s4, r4)
    ig_ref[...] = r4[:, 0].reshape(rows, n).astype(F32).T.astype(BF16)
    fg_ref[...] = r4[:, 1].reshape(rows, n).astype(F32).T
    sent(3, s4, r4)


def local(nb, nchan, inputs, gate, filter_taps, cotangent):
    n, local_chan = inputs.shape
    cb = local_chan // nb
    tables = [jnp.asarray(table) for table in dft_tables(n)]
    vmem = pl.BlockSpec(memory_space=pltpu.VMEM)
    one = pltpu.VMEM((nb, cb, n), BF16)
    two = pltpu.VMEM((nb, 2, cb, n), BF16)
    wide = pltpu.VMEM((nb, cb, n), F32)
    return pl.pallas_call(
        functools.partial(kernel, nb, nchan),
        out_shape=(
            jax.ShapeDtypeStruct((n, local_chan), BF16),
            jax.ShapeDtypeStruct((n, local_chan), BF16),
            jax.ShapeDtypeStruct((n, local_chan), BF16),
            jax.ShapeDtypeStruct((n, local_chan), F32),
        ),
        in_specs=[vmem] * 8,
        out_specs=(vmem,) * 4,
        scratch_shapes=[two, two, one, one, one, one, two, two, pltpu.VMEM((nchan, 2, n), F32)]
        + [wide] * 9
        + [
            pltpu.SemaphoreType.DMA((4, nb)),
            pltpu.SemaphoreType.DMA((4, nb)),
            pltpu.SemaphoreType.DMA((nchan,)),
            pltpu.SemaphoreType.DMA((nchan,)),
        ],
        compiler_params=pltpu.CompilerParams(collective_id=0, has_side_effects=True),
    )(inputs, gate, filter_taps, cotangent, *tables)


def solution(mesh):
    spec = P("ctx", "chan")
    body = functools.partial(local, mesh.shape["ctx"], mesh.shape["chan"])
    return jax.shard_map(
        body, mesh=mesh, in_specs=(spec,) * 4, out_specs=(spec,) * 4, check_vma=False
    )
```

time: 503 us -> 75.8 us (0.15)
  waiting for transfers between devices: 235 us -> 0 us
  other arithmetic: 114 us -> 0 us
  blocking collectives: 102 us -> 0 us
  Pallas kernels: 0 us -> 71.5 us
  matrix products: 25.9 us -> 0 us
  between operations: 13.9 us -> 0.66 us
    all_gather x3 -> x0, waiting for transfers between devices: 234 us -> none  [the longest x1 84.4 us: local(): all_inner = lax.all_gather(d_inner, 'ctx', axis=0, tiled=True)]
    scatter-add x96 -> x0, other arithmetic: 114 us -> none  [the longest x32 39.1 us: owner_advance(): imags = imags.at[target].add(addend[1])]
    psum x1 -> x0, blocking collectives: 102 us -> none  [local(): lax.psum((jnp.sum(mixed * mixed, axis=1), jnp.sum(upstream * mixed, axis=...]
    pallas_call x0 -> x1, Pallas kernels: none -> 71.5 us  [local(): pl.pallas_call(functools.partial(kernel, nb, nchan), out_shape=(jax.Shape...]
    dot_general x12 -> x0, matrix products: 25.9 us -> none  [the longest x3 9.2 us: spectrum(): real_part = jnp.einsum('kn,bnc->bkc', fwd_cos, blocks, precision=HIGHEST)]
  transfers between devices with their start and end apart: 3 -> 0, of which waited for: 3 -> 0; matrix products, arithmetic and copies ran while one was open for 2% -> 0% of each run, Pallas kernels for 0% -> 0%
where the time goes in v1:
time: 75.8 us; the launch traced here: 75.6 us
  Pallas kernels  71.5 us (94%)
  local copies, waits for them, and re-layouts  3.43 us (5%)
    pallas_call x1, Pallas kernels, local(): pl.pallas_call(functools.partial(kernel, nb, nchan), out_shape=(jax.Shape...  71.5 us
    unnamed x10, local copies, waits for them, and re-layouts  3.43 us

profile of v1, /device:TPU:1, one launch (start us, length us, event | category | flops | bytes accessed | tf_op | source)
XLA Modules:
  0.0 75.6 jit_solution(10546259281992991087)
XLA Ops:
  0.6 71.5 %shard_map.111 = (bf16[128,256]{1,0:T(8,128)(2,1)}, bf16[128,256]{1,0:T(8,128)(2,1)}, bf16[128,256]{1,0:T(8,128)(2,1)}, f32[128,256]{1,0:T(8,128)}) custom-call(bf16[128,256]{1,0:T(8,128)(2,1)} %x_ref.1, bf16[128,256]{1,0:T(8,128)(2,1)} %g_ref.1, bf16[128,256]{1,0:T(8,128)(2,1)} %h_ref.1, bf16[128,256]{1,0:T(8,128)(2,1)} %c_ref.1, ...), custom_call_target="tpu_custom_call" | custom-call | tf_op jit(solution)/shard_map/pallas_call | solution.py:265
  72.1 0.0 copy-start.2
  72.1 0.0 copy-start.1
  72.1 1.5 %copy.16 = bf16[128,256]{1,0:T(8,128)(2,1)} copy(bf16[128,256]{1,0:T(8,128)(2,1)} %get-tuple-element.8) | data formatting | bytes 131072
  73.6 0.0 copy-done.2
  73.6 0.0 copy-start
  73.6 0.6 copy.17
  74.3 0.0 copy-done.1
  74.3 0.6 copy.18
  74.9 0.0 copy-done
  74.9 0.7 copy.19
Async XLA Ops:
  72.1 1.5 %copy-start.2 = (bf16[128,256]{1,0:T(8,128)(2,1)S(1)}, bf16[128,256]{1,0:T(8,128)(2,1)}, u32[]{:S(2)}) copy-start(bf16[128,256]{1,0:T(8,128)(2,1)} %get-tuple-element.9) | copy-start | bytes 196612
  72.1 2.2 %copy-start.1 = (bf16[128,256]{1,0:T(8,128)(2,1)S(1)}, bf16[128,256]{1,0:T(8,128)(2,1)}, u32[]{:S(2)}) copy-start(bf16[128,256]{1,0:T(8,128)(2,1)} %get-tuple-element.10) | copy-start | bytes 196612
  73.6 1.3 %copy-start = (f32[128,256]{1,0:T(8,128)S(1)}, f32[128,256]{1,0:T(8,128)}, u32[]{:S(2)}) copy-start(f32[128,256]{1,0:T(8,128)} %get-tuple-element.11) | copy-start | bytes 393220

commit v2 on v1

--- a/solution.py
+++ b/solution.py
@@ -37,13 +37,19 @@
     return split_table(fwd) + split_table(inv)
 
 
+def each(indices, step):
+    for k in indices:
+        step(k, 0)
+
+
 def kernel(
     nb, nchan,
-    x_ref, g_ref, h_ref, c_ref, fhi_ref, flo_ref, ihi_ref, ilo_ref,
+    x_hbm, g_hbm, h_hbm, c_hbm, fhi_hbm, flo_hbm, ihi_hbm, ilo_hbm,
     out_ref, gg_ref, ig_ref, fg_ref,
-    s1, r1, s2, r2, s3, r3, s4, r4, stats,
+    s1, r1, s2, r2, s3, r3, s4, r4, s5, r5, stats,
     xre, xim, kre, kre2, kim, vre, vim, qre, qim,
-    send_sems, recv_sems, stat_send, stat_recv,
+    x_ref, h_ref, g_ref, c_ref, fhi_ref, flo_ref, ihi_ref, ilo_ref,
+    send_sems, recv_sems, stat_send, stat_recv, load_sems,
 ):
     me = lax.axis_index("ctx")
     mc = lax.axis_index("chan")
@@ -52,6 +58,17 @@
     rows = nb * cb
     channels = local_chan * nchan
 
+    side = nb // 2
+    half = lax.div(me, side)
+    slot = lax.rem(me, side)
+    peers = list(range(side, nb)) + list(range(1, side))
+
+    def target(k):
+        return lax.rem(half + k // side, 2) * side + lax.rem(slot + k, side)
+
+    def origin(k):
+        return lax.rem(half + k // side, 2) * side + lax.rem(slot + nb - k, side)
+
     barrier = pltpu.get_barrier_semaphore()
 
     def greet_ctx(k, _):
@@ -66,23 +83,33 @@
         )
         return 0
 
-    lax.fori_loop(1, nb, greet_ctx, 0)
-    lax.fori_loop(1, nchan, greet_chan, 0)
+    each(range(1, nb), greet_ctx)
+    each(range(1, nchan), greet_chan)
+
+    pairs = (
+        (x_hbm, x_ref), (h_hbm, h_ref), (g_hbm, g_ref), (c_hbm, c_ref),
+        (fhi_hbm, fhi_ref), (flo_hbm, flo_ref), (ihi_hbm, ihi_ref), (ilo_hbm, ilo_ref),
+    )
+    loads = [pltpu.make_async_copy(a, b, load_sems.at[i]) for i, (a, b) in enumerate(pairs)]
+    for load in loads:
+        load.start()
 
     def turned(ref):
         return ref[...].astype(F32).T
 
+    loads[0].wait()
+    loads[1].wait()
     s1[:, 0] = turned(x_ref).astype(BF16).reshape(nb, cb, n)
     s1[:, 1] = turned(h_ref).astype(BF16).reshape(nb, cb, n)
     pl.semaphore_wait(barrier, nb + nchan - 2)
 
     def exchange(phase, src, dst, k):
         return pltpu.make_async_remote_copy(
-            src_ref=src.at[lax.rem(me + k, nb)],
+            src_ref=src.at[target(k)],
             dst_ref=dst.at[me],
             send_sem=send_sems.at[phase, k],
             recv_sem=recv_sems.at[phase, k],
-            device_id={"ctx": lax.rem(me + k, nb)},
+            device_id={"ctx": target(k)},
             device_id_type=MESH,
         )
 
@@ -91,16 +118,16 @@
             exchange(phase, src, dst, k).start()
             return 0
 
-        lax.fori_loop(1, nb, step, 0)
+        each(peers, step)
         dst[me] = src[me]
 
     def arrived(phase, src, dst, k):
         return pltpu.make_async_remote_copy(
-            src_ref=src.at[lax.rem(me + nb - k, nb)],
-            dst_ref=dst.at[lax.rem(me + nb - k, nb)],
+            src_ref=src.at[origin(k)],
+            dst_ref=dst.at[origin(k)],
             send_sem=send_sems.at[phase, k],
             recv_sem=recv_sems.at[phase, k],
-            device_id={"ctx": lax.rem(me + nb - k, nb)},
+            device_id={"ctx": origin(k)},
             device_id_type=MESH,
         )
 
@@ -109,14 +136,14 @@
             arrived(phase, src, dst, k).wait_recv()
             return 0
 
-        lax.fori_loop(1, nb, step, 0)
+        each(peers, step)
 
     def sent(phase, src, dst):
         def step(k, _):
             exchange(phase, src, dst, k).wait_send()
             return 0
 
-        lax.fori_loop(1, nb, step, 0)
+        each(peers, step)
 
     lane = lax.broadcasted_iota(jnp.int32, (1, 1, n), 2)
     alternate = jnp.where(lax.rem(lane, 2) == 0, 1.0, -1.0).astype(F32)
@@ -159,6 +186,8 @@
                 qim[: nb - d] += new_im
 
     start_exchange(0, s1, r1)
+    for load in loads[2:]:
+        load.wait()
     gate = turned(g_ref)
     upstream = turned(c_ref)
     finish_exchange(0, s1, r1)
@@ -222,36 +251,46 @@
         stat_copy(k).wait_send()
         return 0
 
-    lax.fori_loop(1, nchan, stat_start, 0)
-    lax.fori_loop(1, nchan, stat_wait, 0)
+    each(range(1, nchan), stat_start)
+    each(range(1, nchan), stat_wait)
     totals = jnp.sum(stats[...], axis=0)
     inv_rms = lax.rsqrt(totals[0:1] / channels + EPSILON)
     d_mixed = inv_rms * upstream - mixed * (inv_rms**3 * totals[1:2] / channels)
     s3[...] = (d_mixed * gate).astype(BF16).reshape(nb, cb, n)
     start_exchange(2, s3, r3)
-    out_ref[...] = (mixed * inv_rms).T.astype(BF16)
-    gg_ref[...] = (d_mixed * convolved).T.astype(BF16)
+    out_ref[...] = (mixed * inv_rms).astype(BF16)
+    gg_ref[...] = (d_mixed * convolved).astype(BF16)
     finish_exchange(2, s3, r3)
 
     d_re, d_im = spectrum(r3[...].reshape(rows, n))
     vre[...] = d_re
     vim[...] = d_im
     correlate()
-    s4[:, 0] = inverse().astype(BF16).reshape(nb, cb, n)
+    s4[...] = inverse().astype(BF16).reshape(nb, cb, n)
+    start_exchange(3, s4, r4)
     set_kernel(xre[...], xim[...])
     vre[: nb - 1] += alternate * vre[1:]
     vim[: nb - 1] += alternate * vim[1:]
     correlate()
-    s4[:, 1] = (inverse() * (1.0 / math.sqrt(nb * n))).astype(BF16).reshape(nb, cb, n)
-    start_exchange(3, s4, r4)
+    s5[...] = (inverse() * (1.0 / math.sqrt(nb * n))).astype(BF16).reshape(nb, cb, n)
+    start_exchange(4, s5, r5)
     sent(0, s1, r1)
     sent(1, s2, r2)
-    lax.fori_loop(1, nchan, stat_sent, 0)
+    each(range(1, nchan), stat_sent)
     sent(2, s3, r3)
     finish_exchange(3, s4, r4)
-    ig_ref[...] = r4[:, 0].reshape(rows, n).astype(F32).T.astype(BF16)
-    fg_ref[...] = r4[:, 1].reshape(rows, n).astype(F32).T
+    ig_ref[...] = r4[...].reshape(rows, n)
+    finish_exchange(4, s5, r5)
+    fg_ref[...] = r5[...].reshape(rows, n)
     sent(3, s4, r4)
+    sent(4, s5, r5)
+
+
+def finish(out_t, gg_t, ig_t, fg_t, out_ref, gg_ref, ig_ref, fg_ref):
+    out_ref[...] = out_t[...].astype(F32).T.astype(BF16)
+    gg_ref[...] = gg_t[...].astype(F32).T.astype(BF16)
+    ig_ref[...] = ig_t[...].astype(F32).T.astype(BF16)
+    fg_ref[...] = fg_t[...].astype(F32).T
 
 
 def local(nb, nchan, inputs, gate, filter_taps, cotangent):
@@ -262,26 +301,36 @@
     one = pltpu.VMEM((nb, cb, n), BF16)
     two = pltpu.VMEM((nb, 2, cb, n), BF16)
     wide = pltpu.VMEM((nb, cb, n), F32)
+    turned = pl.pallas_call(
+        functools.partial(kernel, nb, nchan),
+        out_shape=(jax.ShapeDtypeStruct((local_chan, n), BF16),) * 4,
+        in_specs=[pl.BlockSpec(memory_space=pl.ANY)] * 8,
+        out_specs=(vmem,) * 4,
+        scratch_shapes=[two, two, one, one, one, one, one, one, one, one, pltpu.VMEM((nchan, 2, n), F32)]
+        + [wide] * 9
+        + [pltpu.VMEM((n, local_chan), BF16)] * 4
+        + [pltpu.VMEM((n, 2 * n), BF16)] * 2
+        + [pltpu.VMEM((2 * n, n), BF16)] * 2
+        + [
+            pltpu.SemaphoreType.DMA((5, nb)),
+            pltpu.SemaphoreType.DMA((5, nb)),
+            pltpu.SemaphoreType.DMA((nchan,)),
+            pltpu.SemaphoreType.DMA((nchan,)),
+            pltpu.SemaphoreType.DMA((8,)),
+        ],
+        compiler_params=pltpu.CompilerParams(collective_id=0, has_side_effects=True),
+    )(inputs, gate, filter_taps, cotangent, *tables)
     return pl.pallas_call(
-        functools.partial(kernel, nb, nchan),
+        finish,
         out_shape=(
             jax.ShapeDtypeStruct((n, local_chan), BF16),
             jax.ShapeDtypeStruct((n, local_chan), BF16),
             jax.ShapeDtypeStruct((n, local_chan), BF16),
             jax.ShapeDtypeStruct((n, local_chan), F32),
         ),
-        in_specs=[vmem] * 8,
+        in_specs=[vmem] * 4,
         out_specs=(vmem,) * 4,
-        scratch_shapes=[two, two, one, one, one, one, two, two, pltpu.VMEM((nchan, 2, n), F32)]
-        + [wide] * 9
-        + [
-            pltpu.SemaphoreType.DMA((4, nb)),
-            pltpu.SemaphoreType.DMA((4, nb)),
-            pltpu.SemaphoreType.DMA((nchan,)),
-            pltpu.SemaphoreType.DMA((nchan,)),
-        ],
-        compiler_params=pltpu.CompilerParams(collective_id=0, has_side_effects=True),
-    )(inputs, gate, filter_taps, cotangent, *tables)
+    )(*turned)
 
 
 def solution(mesh):

time: 75.8 us -> 73.8 us (0.974)
  local copies, waits for them, and re-layouts: 3.43 us -> 0 us
  Pallas kernels: 71.5 us -> 73 us
    unnamed x10 -> x0, local copies, waits for them, and re-layouts: 3.43 us -> none
    pallas_call x0 -> x1, Pallas kernels: none -> 1.76 us  [local(): pl.pallas_call(finish, out_shape=(jax.ShapeDtypeStruct((n, local_chan), B...]
where the time goes in v2:
time: 73.8 us; the launch traced here: 73.6 us
  Pallas kernels  73 us (99%)
    pallas_call x1, Pallas kernels, local(): pl.pallas_call(functools.partial(kernel, nb, nchan), out_shape=(jax.Shape...  71.2 us
    pallas_call x1, Pallas kernels, local(): pl.pallas_call(finish, out_shape=(jax.ShapeDtypeStruct((n, local_chan), B...  1.76 us

profile of v2, /device:TPU:1, one launch (start us, length us, event | category | flops | bytes accessed | tf_op | source)
XLA Modules:
  0.0 73.6 jit_solution(14848624580394278272)
XLA Ops:
  0.6 71.2 %shard_map.111 = (bf16[256,128]{1,0:T(8,128)(2,1)}, bf16[256,128]{1,0:T(8,128)(2,1)}, bf16[256,128]{1,0:T(8,128)(2,1)}, bf16[256,128]{1,0:T(8,128)(2,1)}) custom-call(bf16[128,256]{1,0:T(8,128)(2,1)} %x_hbm.1, bf16[128,256]{1,0:T(8,128)(2,1)} %g_hbm.1, bf16[128,256]{1,0:T(8,128)(2,1)} %h_hbm.1, bf16[128,256]{1,0:T(8,128)(2,1)} %c_hbm.1, ...), custom_call_target="tpu_custom_call" | custom-call | tf_op jit(solution)/shard_map/pallas_call | solution.py:304
  71.9 1.8 %shard_map.112 = (bf16[128,256]{1,0:T(8,128)(2,1)}, bf16[128,256]{1,0:T(8,128)(2,1)}, bf16[128,256]{1,0:T(8,128)(2,1)}, f32[128,256]{1,0:T(8,128)}) custom-call(bf16[256,128]{1,0:T(8,128)(2,1)} %get-tuple-element.8.out_t, bf16[256,128]{1,0:T(8,128)(2,1)} %get-tuple-element.9.gg_t, bf16[256,128]{1,0:T(8,128)(2,1)} %get-tuple-element.10.ig_t, ...), custom_call_target="tpu_custom_call" | custom-call | tf_op jit(solution)/shard_map/pallas_call | solution.py:323

commit v3 on v2

--- a/solution.py
+++ b/solution.py
@@ -251,7 +251,7 @@
         stat_copy(k).wait_send()
         return 0
 
-    each(range(1, nchan), stat_start)
+    each(sorted(range(1, nchan), key=lambda k: abs(k % 8 - 4)), stat_start)
     each(range(1, nchan), stat_wait)
     totals = jnp.sum(stats[...], axis=0)
     inv_rms = lax.rsqrt(totals[0:1] / channels + EPSILON)

time: 73.8 us -> 73.8 us (level)
  no operation moved by 1% of the time
where the time goes in v3:
time: 73.8 us; the launch traced here: 73.6 us
  Pallas kernels  73 us (99%)
    pallas_call x1, Pallas kernels, local(): pl.pallas_call(functools.partial(kernel, nb, nchan), out_shape=(jax.Shape...  71.2 us
    pallas_call x1, Pallas kernels, local(): pl.pallas_call(finish, out_shape=(jax.ShapeDtypeStruct((n, local_chan), B...  1.76 us

profile of v3, /device:TPU:1, one launch (start us, length us, event | category | flops | bytes accessed | tf_op | source)
XLA Modules:
  0.0 73.6 jit_solution(2434277682535612231)
XLA Ops:
  0.6 71.2 %shard_map.111 = (bf16[256,128]{1,0:T(8,128)(2,1)}, bf16[256,128]{1,0:T(8,128)(2,1)}, bf16[256,128]{1,0:T(8,128)(2,1)}, bf16[256,128]{1,0:T(8,128)(2,1)}) custom-call(bf16[128,256]{1,0:T(8,128)(2,1)} %x_hbm.1, bf16[128,256]{1,0:T(8,128)(2,1)} %g_hbm.1, bf16[128,256]{1,0:T(8,128)(2,1)} %h_hbm.1, bf16[128,256]{1,0:T(8,128)(2,1)} %c_hbm.1, ...), custom_call_target="tpu_custom_call" | custom-call | tf_op jit(solution)/shard_map/pallas_call | solution.py:304
  71.8 1.8 %shard_map.112 = (bf16[128,256]{1,0:T(8,128)(2,1)}, bf16[128,256]{1,0:T(8,128)(2,1)}, bf16[128,256]{1,0:T(8,128)(2,1)}, f32[128,256]{1,0:T(8,128)}) custom-call(bf16[256,128]{1,0:T(8,128)(2,1)} %get-tuple-element.8.out_t, bf16[256,128]{1,0:T(8,128)(2,1)} %get-tuple-element.9.gg_t, bf16[256,128]{1,0:T(8,128)(2,1)} %get-tuple-element.10.ig_t, ...), custom_call_target="tpu_custom_call" | custom-call | tf_op jit(solution)/shard_map/pallas_call | solution.py:323
